TPU v7x, 32 devices: a whole 2x2x4 slice. The times are simulated.
32 devices in a mesh: pipe: 2 (over x), expert: 16 (over z, y, core).
Axes of the slice: x: 2, y: 2, z: 4, core: 2. Of those that a mesh axis runs over, the one named last changes fastest.
Arguments:
- front_tokens: bfloat16 [2, 192, 3584], P('pipe', 'expert'), may hold values from -6 to 6
- front_routes: int32 [2, 192, 2], P('pipe', 'expert'), may hold values from 0 to 1, all different within a row; in each aligned block of 12 rows (0 to 11, 12 to 23, ..., all dimensions but the last counted through in order) at most 12 rows name the same one
- front_mixing: int32 [2, 192, 2], P('pipe', 'expert'), may hold values from 1 to 15
- back_tokens: bfloat16 [2, 192, 3584], P('pipe', 'expert'), may hold values from -6 to 6
- back_routes: int32 [2, 192, 2], P('pipe', 'expert'), may hold values from 0 to 1, all different within a row; in each aligned block of 12 rows (0 to 11, 12 to 23, ..., all dimensions but the last counted through in order) at most 12 rows name the same one
- back_mixing: int32 [2, 192, 2], P('pipe', 'expert'), may hold values from 1 to 15
- back_upstream: bfloat16 [2, 192, 3584], P('pipe', 'expert'), may hold values from -6 to 6
- gate_weight: bfloat16 [2, 3584, 2048], P('pipe', None, 'expert'), may hold values from -0.09375 to 0.09375
- up_weight: bfloat16 [2, 3584, 2048], P('pipe', None, 'expert'), may hold values from -0.09375 to 0.09375
- down_weight: bfloat16 [2, 2048, 3584], P('pipe', 'expert'), may hold values from -0.1875 to 0.1875
Outputs:
- front_result: bfloat16 [2, 192, 3584], P('pipe', 'expert')
- token_grads: bfloat16 [2, 192, 3584], P('pipe', 'expert')
- gate_grads: bfloat16 [2, 1792, 2048], P('pipe', None, 'expert')
- up_grads: bfloat16 [2, 1792, 2048], P('pipe', None, 'expert')
- down_grads: bfloat16 [2, 2048, 1792], P('pipe', 'expert')
Inputs may be any that keep to these rules, and one draw needn't show every extreme that they name: `front_routes`: each row names 2 different experts; within each device's block of 12 rows no expert is named more than 12 times, a bound that some block reaches. `back_routes`: each row names 2 different experts; within each device's block of 12 rows no expert is named more than 12 times, a bound that some block reaches.
All inputs are finite; a program needn't handle non-finite values.
Results may differ from a plain program's by a relative error of at most 0.0071.
Values may be sent and summed in bfloat16 or wider, within the bound.
A program may use at most 64 MiB of HBM per device.

v0:
```python
import jax
import jax.numpy as jnp
from jax import lax
from jax.sharding import PartitionSpec as P

SHARDS = 8
weight_unit = 0.0625


def hit_tables(routes, mixing, experts, capacity):
    token_count, route_count = routes.shape
    flat_routes = routes.reshape(token_count * route_count)
    matches = (flat_routes[:, None] == jnp.arange(experts, dtype=jnp.int32)[None, :]).astype(
        jnp.int32
    )
    earlier = jnp.cumsum(matches, axis=0) - matches
    position = jnp.sum(earlier * matches, axis=1)
    slot_ids = flat_routes * capacity + position
    hit_table = (
        slot_ids[:, None] == jnp.arange(experts * capacity, dtype=jnp.int32)[None, :]
    ).astype(jnp.float32)
    hit_table = hit_table.reshape(token_count, route_count, experts * capacity)
    weights = mixing.astype(jnp.float32) * weight_unit
    picker = jnp.sum(hit_table, axis=1)
    mix_table = jnp.sum(hit_table * weights[:, :, None], axis=1)
    return (picker, mix_table)


def deliver(slot_rows, experts, capacity):
    stacks = slot_rows.shape[0]
    feature_count = slot_rows.shape[2]
    copies = jnp.repeat(slot_rows.reshape(stacks, experts, capacity, feature_count), SHARDS, axis=1)
    landed = lax.all_to_all(copies, "expert", split_axis=1, concat_axis=1, tiled=True)
    return landed.reshape(stacks, experts * SHARDS * capacity, feature_count)


def collect(shard_parts, experts, capacity):
    feature_count = shard_parts.shape[1]
    sources = experts * SHARDS
    returned = lax.all_to_all(
        shard_parts.reshape(sources, capacity, feature_count),
        "expert",
        split_axis=0,
        concat_axis=0,
        tiled=True,
    )
    summed = jnp.sum(
        returned.reshape(experts, SHARDS, capacity, feature_count).astype(jnp.float32), axis=1
    )
    result_rows = summed.astype(jnp.bfloat16).reshape(experts * capacity, feature_count)
    return result_rows


def mirror_move(values, split_dim, concat_dim):
    return lax.all_to_all(values, "pipe", split_axis=split_dim, concat_axis=concat_dim, tiled=True)


def local(
    front_tokens,
    front_routes,
    front_mixing,
    back_tokens,
    back_routes,
    back_mixing,
    back_upstream,
    gate_weight,
    up_weight,
    down_weight,
):
    experts = lax.axis_size("expert") // SHARDS
    token_count = front_tokens.shape[1]
    route_count = front_routes.shape[2]
    feature_count = front_tokens.shape[2]
    capacity = min(token_count, max(2, 3 * token_count * route_count // (2 * experts)))
    front_pick, front_mix = hit_tables(front_routes[0], front_mixing[0], experts, capacity)
    back_pick, back_mix = hit_tables(back_routes[0], back_mixing[0], experts, capacity)
    front_slots = jnp.dot(
        front_pick.T.astype(jnp.bfloat16), front_tokens[0], preferred_element_type=jnp.float32
    ).astype(jnp.bfloat16)
    back_slots = jnp.dot(
        back_pick.T.astype(jnp.bfloat16), back_tokens[0], preferred_element_type=jnp.float32
    ).astype(jnp.bfloat16)
    scaled_slots = jnp.dot(
        back_mix.T, back_upstream[0].astype(jnp.float32), precision=lax.Precision.HIGHEST
    ).astype(jnp.bfloat16)
    landed = deliver(jnp.stack([front_slots, back_slots, scaled_slots]), experts, capacity)
    gate_cols = gate_weight[0]
    up_cols = up_weight[0]
    down_rows = down_weight[0]
    front_rows = landed[0]
    front_gate = jnp.dot(front_rows, gate_cols, preferred_element_type=jnp.float32)
    front_up = jnp.dot(front_rows, up_cols, preferred_element_type=jnp.float32)
    front_hidden = (jax.nn.silu(front_gate) * front_up).astype(jnp.bfloat16)
    front_parts = jnp.dot(front_hidden, down_rows, preferred_element_type=jnp.float32).astype(
        jnp.bfloat16
    )
    front_summed = collect(front_parts, experts, capacity)
    front_result = jnp.dot(
        front_mix, front_summed.astype(jnp.float32), precision=lax.Precision.HIGHEST
    ).astype(jnp.bfloat16)
    back_rows = landed[1]
    scaled_rows = landed[2]
    back_gate = jnp.dot(back_rows, gate_cols, preferred_element_type=jnp.float32)
    back_up = jnp.dot(back_rows, up_cols, preferred_element_type=jnp.float32)
    gate_act = jax.nn.silu(back_gate)
    gate_sig = jax.nn.sigmoid(back_gate)
    back_hidden = (gate_act * back_up).astype(jnp.bfloat16)
    down_section = jnp.dot(scaled_rows.T, back_hidden, preferred_element_type=jnp.float32).astype(
        jnp.bfloat16
    )
    hidden_grad = jnp.dot(scaled_rows, down_rows.T, preferred_element_type=jnp.float32)
    act_slope = gate_sig * (1.0 + back_gate * (1.0 - gate_sig))
    gate_delta = (hidden_grad * back_up * act_slope).astype(jnp.bfloat16)
    up_delta = (hidden_grad * gate_act).astype(jnp.bfloat16)
    gate_section = jnp.dot(back_rows.T, gate_delta, preferred_element_type=jnp.float32).astype(
        jnp.bfloat16
    )
    up_section = jnp.dot(back_rows.T, up_delta, preferred_element_type=jnp.float32).astype(
        jnp.bfloat16
    )
    back_parts = (
        jnp.dot(gate_delta, gate_cols.T, preferred_element_type=jnp.float32)
        + jnp.dot(up_delta, up_cols.T, preferred_element_type=jnp.float32)
    ).astype(jnp.bfloat16)
    grad_slots = collect(back_parts, experts, capacity)
    token_grads = jnp.dot(
        back_pick.astype(jnp.bfloat16), grad_slots, preferred_element_type=jnp.float32
    ).astype(jnp.bfloat16)
    section_grads = lax.optimization_barrier(jnp.stack([gate_section, up_section, down_section]))
    pipe_count = lax.axis_size("pipe")
    half_rows = feature_count // 2
    upper_half = lax.axis_index("pipe") * 2 >= pipe_count
    own_half = jnp.where(upper_half, section_grads[:, half_rows:], section_grads[:, :half_rows])
    leaving = jnp.where(upper_half, section_grads[:, :half_rows], section_grads[:, half_rows:])
    piece_rows = half_rows // pipe_count
    spread_out = mirror_move(leaving, 1, 0)
    by_source = spread_out.reshape(pipe_count, 3, piece_rows, leaving.shape[2])
    reversed_sources = jnp.flip(by_source, axis=0).reshape(
        pipe_count * 3, piece_rows, leaving.shape[2]
    )
    leaving = mirror_move(reversed_sources, 0, 1)
    summed = (own_half.astype(jnp.float32) + leaving.astype(jnp.float32)).astype(jnp.bfloat16)
    return (
        front_result[None],
        token_grads[None],
        summed[0][None],
        summed[1][None],
        summed[2].T[None],
    )


def solution(mesh):
    placed = (
        P("pipe", "expert", None),
        P("pipe", "expert", None),
        P("pipe", "expert", None),
        P("pipe", "expert", None),
        P("pipe", "expert", None),
        P("pipe", "expert", None),
        P("pipe", "expert", None),
        P("pipe", None, "expert"),
        P("pipe", None, "expert"),
        P("pipe", "expert", None),
    )
    return jax.shard_map(
        local,
        mesh=mesh,
        in_specs=placed,
        out_specs=(
            P("pipe", "expert", None),
            P("pipe", "expert", None),
            P("pipe", None, "expert"),
            P("pipe", None, "expert"),
            P("pipe", "expert", None),
        ),
        check_vma=False,
    )
```

profile of v0, /device:TPU:13, one launch (start us, length us, event | category | flops | bytes accessed | tf_op | source)
XLA Modules:
  0.0 313.1 jit_solution(14618682792077326766)
XLA Ops:
  0.7 0.9 copy.61
  1.5 0.1 eq.58
  1.7 0.2 select_reduce_fusion.3
  2.0 0.1 copy.62
  2.1 0.7 bitcast_add_fusion.2
  2.8 0.1 copy.63
  2.9 0.7 multiply_bitcast_fusion.1
  3.6 0.1 copy.64
  3.7 0.8 copy.65
  4.6 0.2 select_reduce_fusion.1
  4.9 0.1 copy.66
  5.0 0.7 bitcast_add_fusion.1
  5.7 0.1 copy.67
  5.8 0.7 multiply_bitcast_fusion
  6.5 0.1 copy.68
  6.6 0.1 convert_reduce_fusion
  6.7 1.2 convolution_convert_fusion.4
  8.0 1.1 convolution_convert_fusion.5
  9.2 0.1 convert_reduce_fusion.1
  9.3 0.2 convolution_convert_fusion.6
  9.6 0.1 pad_maximum_fusion.1
  9.8 3.1 broadcast_in_dim.8
  12.9 6.6 %all-to-all-start = ((bf16[3,16,12,3584]{3,2,0,1:T(8,128)(2,1)}), bf16[3,16,12,3584]{3,2,0,1:T(8,128)(2,1)}, u32[]{:S(2)}, u32[]{:S(2)}) async-start(bf16[3,16,12,3584]{3,2,0,1:T(8,128)(2,1)} %bitcast.97), calls=%async_computation | async-start | bytes 11010048 | tf_op jit(solution)/shard_map/all_to_all | solution.py:33
  19.4 120.6 %all-to-all-done = bf16[3,16,12,3584]{3,2,0,1:T(8,128)(2,1)} async-done(((bf16[3,16,12,3584]{3,2,0,1:T(8,128)(2,1)}), bf16[3,16,12,3584]{3,2,0,1:T(8,128)(2,1)}, u32[]{:S(2)}, u32[]{:S(2)}) %all-to-all-start) | async-done | bytes 4128800 | tf_op jit(solution)/shard_map/all_to_all | solution.py:33
  140.0 5.2 %fusion.40 = (bf16[1,16,12,3584]{3,2,0,1:T(8,128)(2,1)}, bf16[1,16,12,3584]{3,2,0,1:T(8,128)(2,1)}, bf16[1,16,12,3584]{3,2,0,1:T(8,128)(2,1)}) fusion(bf16[3,16,12,3584]{3,2,0,1:T(8,128)(2,1)} %all-to-all-done), kind=kLoop, calls=%fused_computation.75 | loop fusion | bytes 8257536 | tf_op jit(solution)/shard_map/slice | solution.py:102
  145.2 2.4 squeeze.40
  147.6 0.5 fusion.18
  148.1 0.5 fusion.12
  148.7 3.4 %squeeze.39 = bf16[192,3584]{1,0:T(8,128)(2,1)} reshape(bf16[1,16,12,3584]{3,2,0,1:T(8,128)(2,1)} %get-tuple-element.34) | data formatting | bytes 2752512 | tf_op jit(solution)/shard_map/squeeze | solution.py:102
  152.1 2.2 fusion.3
  154.3 0.5 multiply_convert_fusion.1
  154.8 0.7 fusion.2
  155.5 0.7 fusion.1
  156.3 0.3 pad_maximum_fusion
  156.6 0.1 broadcast_select_fusion
  156.7 1.4 copy-done.1
  158.1 8.5 %copy.70 = bf16[3,1792,128]{2,0,1:T(4,128)(2,1)S(1)} copy(bf16[3,1792,128]{2,1,0:T(8,128)(2,1)S(1)} %broadcast_select_fusion) | data formatting | bytes 2752512 | tf_op jit(solution)/shard_map/jit(_where)/select_n | solution.py:134
  166.6 24.4 %all_to_all.39 = bf16[3,1792,128]{2,0,1:T(4,128)(2,1)S(1)} all-to-all(bf16[3,1792,128]{2,0,1:T(4,128)(2,1)S(1)} %copy.70), channel_id=1, replica_groups=mesh['pipe'=2,'expert'=16] {'pipe'}, dimensions={1} | all-to-all | bytes 2752512 | tf_op jit(solution)/shard_map/all_to_all | solution.py:55
  191.1 0.2 copy.71
  191.3 1.2 reverse.3
  192.5 2.5 copy.72
  195.0 4.8 %all-to-all-start.4 = ((bf16[6,896,128]{2,1,0:T(8,128)(2,1)}), bf16[6,896,128]{2,1,0:T(8,128)(2,1)}, u32[]{:S(2)}, u32[]{:S(2)}) async-start(bf16[6,896,128]{2,1,0:T(8,128)(2,1)} %bitcast.20), calls=%async_computation.4 | async-start | bytes 2752512 | tf_op jit(solution)/shard_map/all_to_all | solution.py:55
  199.7 2.4 squeeze.35
  202.1 0.5 fusion.20
  202.6 3.2 %convolution_convert_fusion = bf16[192,3584]{1,0:T(8,128)(2,1)} fusion(bf16[192,3584]{1,0:T(8,128)(2,1)S(1)} %squeeze.35, bf16[1,128,3584]{2,1,0:T(8,128)(2,1)} %param.19, bf16[1,3584,128]{2,1,0:T(8,128)(2,1)S(1)} %copy-done, f32[192,128]{1,0:T(8,128)S(1)} %fusion.20), kind=kOutput, calls=%fused_computation.2 | convolution fusion | flops 353157120 | bytes 4685824 | tf_op jit(solution)/shard_map/dot_general | solution.py:94
  205.9 3.3 %reshape.117 = bf16[16,12,3584]{2,1,0:T(8,128)(2,1)} reshape(bf16[192,3584]{1,0:T(8,128)(2,1)} %convolution_convert_fusion) | data formatting | bytes 2752512 | tf_op jit(solution)/shard_map/reshape | solution.py:41
  209.1 6.6 %all-to-all-done.4 = bf16[6,896,128]{2,1,0:T(8,128)(2,1)} async-done(((bf16[6,896,128]{2,1,0:T(8,128)(2,1)}), bf16[6,896,128]{2,1,0:T(8,128)(2,1)}, u32[]{:S(2)}, u32[]{:S(2)}) %all-to-all-start.4) | async-done | bytes 1376288 | tf_op jit(solution)/shard_map/all_to_all | solution.py:55
  215.7 6.7 %all-to-all-start.1 = ((bf16[16,12,3584]{2,1,0:T(8,128)(2,1)}), bf16[16,12,3584]{2,1,0:T(8,128)(2,1)}, u32[]{:S(2)}, u32[]{:S(2)}) async-start(bf16[16,12,3584]{2,1,0:T(8,128)(2,1)} %reshape.117), calls=%async_computation.1 | async-start | bytes 3670016 | tf_op jit(solution)/shard_map/all_to_all | solution.py:40
  222.4 0.5 fusion.16
  222.9 0.5 fusion
  223.5 1.4 reshape.120
  224.9 39.4 %all-to-all-done.1 = bf16[16,12,3584]{2,1,0:T(8,128)(2,1)} async-done(((bf16[16,12,3584]{2,1,0:T(8,128)(2,1)}), bf16[16,12,3584]{2,1,0:T(8,128)(2,1)}, u32[]{:S(2)}, u32[]{:S(2)}) %all-to-all-start.1) | async-done | bytes 1376288 | tf_op jit(solution)/shard_map/all_to_all | solution.py:40
  264.3 4.9 %all-to-all-start.2 = ((bf16[16,12,3584]{2,1,0:T(8,128)(2,1)}), bf16[16,12,3584]{2,1,0:T(8,128)(2,1)S(1)}, u32[]{:S(2)}, u32[]{:S(2)}) async-start(bf16[16,12,3584]{2,1,0:T(8,128)(2,1)} %reshape.120), calls=%async_computation.2 | async-start | bytes 3670016 | tf_op jit(solution)/shard_map/all_to_all | solution.py:40
  269.2 1.5 convert_bitcast_fusion
  270.8 0.2 copy.73
  271.0 1.6 copy-done.2
  272.5 0.4 fusion.6
  273.0 1.0 slice_bitcast_fusion
  274.0 1.0 copy.74
  275.0 1.8 bitcast_reduce_fusion.1
  276.8 34.2 %all-to-all-done.2 = bf16[16,12,3584]{2,1,0:T(8,128)(2,1)S(1)} async-done(((bf16[16,12,3584]{2,1,0:T(8,128)(2,1)}), bf16[16,12,3584]{2,1,0:T(8,128)(2,1)S(1)}, u32[]{:S(2)}, u32[]{:S(2)}) %all-to-all-start.2) | async-done | bytes 1376288 | tf_op jit(solution)/shard_map/all_to_all | solution.py:40
  311.0 0.3 bitcast_reduce_fusion
  311.4 0.8 fusion.5
  312.2 0.9 fusion.4
  (25 shorter events, 0.8 us)
Async XLA Ops:
  0.6 147.5 %copy-start = (bf16[1,3584,128]{2,1,0:T(8,128)(2,1)S(1)}, bf16[1,3584,128]{2,1,0:T(8,128)(2,1)}, u32[]{:S(2)}) copy-start(bf16[1,3584,128]{2,1,0:T(8,128)(2,1)} %param.18) | copy-start | bytes 2752516
  0.6 8.7 %copy-start.6 = (bf16[1,12,3584]{2,1,0:T(8,128)(2,1)S(1)}, bf16[1,12,3584]{2,1,0:T(8,128)(2,1)}, u32[]{:S(2)}) copy-start(bf16[1,12,3584]{2,1,0:T(8,128)(2,1)} %param.10) | copy-start | bytes 258052
  12.9 127.1 %all-to-all-start = ((bf16[3,16,12,3584]{3,2,0,1:T(8,128)(2,1)}), bf16[3,16,12,3584]{3,2,0,1:T(8,128)(2,1)}, u32[]{:S(2)}, u32[]{:S(2)}) async-start(bf16[3,16,12,3584]{3,2,0,1:T(8,128)(2,1)} %bitcast.97), calls=%async_computation | async-start | bytes 11010048 | tf_op jit(solution)/shard_map/all_to_all | solution.py:33
  145.2 2.5 copy-start.3
  152.1 2.2 copy-start.4
  152.1 2.2 copy-start.5
  156.6 1.6 copy-start.1
  195.0 20.8 %all-to-all-start.4 = ((bf16[6,896,128]{2,1,0:T(8,128)(2,1)}), bf16[6,896,128]{2,1,0:T(8,128)(2,1)}, u32[]{:S(2)}, u32[]{:S(2)}) async-start(bf16[6,896,128]{2,1,0:T(8,128)(2,1)} %bitcast.20), calls=%async_computation.4 | async-start | bytes 2752512 | tf_op jit(solution)/shard_map/all_to_all | solution.py:55
  215.7 48.6 %all-to-all-start.1 = ((bf16[16,12,3584]{2,1,0:T(8,128)(2,1)}), bf16[16,12,3584]{2,1,0:T(8,128)(2,1)}, u32[]{:S(2)}, u32[]{:S(2)}) async-start(bf16[16,12,3584]{2,1,0:T(8,128)(2,1)} %reshape.117), calls=%async_computation.1 | async-start | bytes 3670016 | tf_op jit(solution)/shard_map/all_to_all | solution.py:40
  264.3 46.7 %all-to-all-start.2 = ((bf16[16,12,3584]{2,1,0:T(8,128)(2,1)}), bf16[16,12,3584]{2,1,0:T(8,128)(2,1)S(1)}, u32[]{:S(2)}, u32[]{:S(2)}) async-start(bf16[16,12,3584]{2,1,0:T(8,128)(2,1)} %reshape.120), calls=%async_computation.2 | async-start | bytes 3670016 | tf_op jit(solution)/shard_map/all_to_all | solution.py:40
  270.8 1.8 copy-start.2
where the time goes:
time: 314 us; the launch traced here: 313 us
  waiting for transfers between devices  201 us (64%)
  local copies, waits for them, and re-layouts  41.6 us (13%)
  blocking collectives  24.4 us (8%)
  starting transfers between devices  22.9 us (7%)
  matrix products  14.2 us (5%)
  other arithmetic  8.21 us (3%)
    all_to_all x1, waiting for transfers between devices, deliver(): lax.all_to_all(copies, 'expert', split_axis=1, concat_axis=1, tiled=True)  121 us
    all_to_all x2, waiting for transfers between devices, collect(): lax.all_to_all(shard_parts.reshape(sources, capacity, feature_count), 'ex...  73.6 us
    all_to_all x1, blocking collectives, mirror_move(): lax.all_to_all(values, 'pipe', split_axis=split_dim, concat_axis=concat_d...  24.4 us
    all_to_all x2, starting transfers between devices, collect(): lax.all_to_all(shard_parts.reshape(sources, capacity, feature_count), 'ex...  11.6 us
    select_n x1, local copies, waits for them, and re-layouts, local(): jnp.where(upper_half, section_grads[:, :half_rows], section_grads[:, half...  8.52 us
    all_to_all x1, waiting for transfers between devices, mirror_move(): lax.all_to_all(values, 'pipe', split_axis=split_dim, concat_axis=concat_d...  6.6 us
    all_to_all x1, starting transfers between devices, deliver(): lax.all_to_all(copies, 'expert', split_axis=1, concat_axis=1, tiled=True)  6.55 us
  transfers between devices with their start and end apart: 4, of which 4 were waited for; matrix products, arithmetic and copies ran while one was open for 6% of the time, Pallas kernels for 0%

commit v1 on v0

--- a/solution.py
+++ b/solution.py
@@ -5,6 +5,12 @@
 
 SHARDS = 8
 weight_unit = 0.0625
+
+
+def stacked_exchange(shard, mesh_axis, split, join):
+    cells = jnp.split(shard, lax.axis_size(mesh_axis), axis=split)
+    arrived = lax.all_to_all(jnp.stack(cells), mesh_axis, 0, 0)
+    return jnp.concatenate(arrived, axis=join)
 
 
 def hit_tables(routes, mixing, experts, capacity):
@@ -30,7 +36,7 @@
     stacks = slot_rows.shape[0]
     feature_count = slot_rows.shape[2]
     copies = jnp.repeat(slot_rows.reshape(stacks, experts, capacity, feature_count), SHARDS, axis=1)
-    landed = lax.all_to_all(copies, "expert", split_axis=1, concat_axis=1, tiled=True)
+    landed = stacked_exchange(copies, "expert", 1, 1)
     return landed.reshape(stacks, experts * SHARDS * capacity, feature_count)
 
 

time: 314 us -> 325 us (1.035)
  local copies, waits for them, and re-layouts: 41.6 us -> 50 us
    unnamed x17 -> x26, local copies, waits for them, and re-layouts: 5.63 us -> 15.7 us
where the time goes in v1:
time: 325 us; the launch traced here: 324 us
  waiting for transfers between devices  201 us (62%)
  local copies, waits for them, and re-layouts  50 us (15%)
  blocking collectives  24.4 us (8%)
  starting transfers between devices  22.9 us (7%)
  matrix products  16.5 us (5%)
  other arithmetic  8.21 us (3%)
    all_to_all x1, waiting for transfers between devices, stacked_exchange(): arrived = lax.all_to_all(jnp.stack(cells), mesh_axis, 0, 0)  121 us
    all_to_all x2, waiting for transfers between devices, collect(): lax.all_to_all(shard_parts.reshape(sources, capacity, feature_count), 'ex...  73.6 us
    all_to_all x1, blocking collectives, mirror_move(): lax.all_to_all(values, 'pipe', split_axis=split_dim, concat_axis=concat_d...  24.4 us
    unnamed x26, local copies, waits for them, and re-layouts  15.7 us
    all_to_all x2, starting transfers between devices, collect(): lax.all_to_all(shard_parts.reshape(sources, capacity, feature_count), 'ex...  11.6 us
    select_n x1, local copies, waits for them, and re-layouts, local(): jnp.where(upper_half, section_grads[:, :half_rows], section_grads[:, half...  8.54 us
    all_to_all x1, waiting for transfers between devices, mirror_move(): lax.all_to_all(values, 'pipe', split_axis=split_dim, concat_axis=concat_d...  6.77 us
    all_to_all x1, starting transfers between devices, stacked_exchange(): arrived = lax.all_to_all(jnp.stack(cells), mesh_axis, 0, 0)  6.56 us
  transfers between devices with their start and end apart: 4, of which 4 were waited for; matrix products, arithmetic and copies ran while one was open for 6% of the time, Pallas kernels for 0%

profile of v1, /device:TPU:13, one launch (start us, length us, event | category | flops | bytes accessed | tf_op | source)
XLA Modules:
  0.0 324.0 jit_solution(129643829297920425)
XLA Ops:
  0.6 0.8 copy.122
  2.1 0.7 bitcast_add_fusion.2
  2.9 0.7 multiply_bitcast_fusion.1
  3.6 0.8 copy.126
  5.0 0.7 bitcast_add_fusion.1
  5.8 0.7 multiply_bitcast_fusion
  6.7 1.2 convolution_convert_fusion.4
  8.0 1.1 convolution_convert_fusion.5
  9.3 1.1 convolution_convert_fusion.6
  10.6 0.6 broadcast_in_dim.8
  11.3 0.8 fusion.37
  12.1 0.7 fusion.36
  12.8 0.8 fusion.35
  13.6 0.8 fusion.34
  14.3 0.8 fusion.33
  15.1 0.8 fusion.32
  15.8 0.7 fusion.31
  16.6 0.8 fusion.30
  17.3 0.8 fusion.29
  18.1 0.8 fusion.28
  18.9 0.8 fusion.27
  19.7 0.8 fusion.26
  20.5 0.8 fusion.25
  21.2 0.7 fusion.24
  22.0 0.8 fusion.23
  22.8 0.8 fusion.22
  23.5 6.6 %all-to-all-start = ((bf16[16,3,1,12,3584]{4,3,2,1,0:T(8,128)(2,1)}), bf16[16,3,1,12,3584]{4,3,2,1,0:T(8,128)(2,1)}, u32[]{:S(2)}, u32[]{:S(2)}) async-start(bf16[16,3,1,12,3584]{4,3,2,1,0:T(8,128)(2,1)} %fusion.22), calls=%async_computation | async-start | bytes 11010048 | tf_op jit(solution)/shard_map/all_to_all | solution.py:12
  30.1 120.6 %all-to-all-done = bf16[16,3,1,12,3584]{4,3,2,1,0:T(8,128)(2,1)} async-done(((bf16[16,3,1,12,3584]{4,3,2,1,0:T(8,128)(2,1)}), bf16[16,3,1,12,3584]{4,3,2,1,0:T(8,128)(2,1)}, u32[]{:S(2)}, u32[]{:S(2)}) %all-to-all-start) | async-done | bytes 4128800 | tf_op jit(solution)/shard_map/all_to_all | solution.py:12
  150.7 5.2 %fusion.56 = (bf16[1,16,1,12,3584]{4,3,2,0,1:T(8,128)(2,1)}, bf16[1,16,1,12,3584]{4,3,2,0,1:T(8,128)(2,1)}, bf16[1,16,1,12,3584]{4,3,2,0,1:T(8,128)(2,1)}) fusion(bf16[3,16,1,12,3584]{4,3,2,0,1:T(8,128)(2,1)} %bitcast.39), kind=kLoop, calls=%fused_computation.107 | loop fusion | bytes 8257536 | tf_op jit(solution)/shard_map/slice | solution.py:108
  155.8 2.4 squeeze.40
  158.3 0.5 fusion.18
  158.8 0.5 fusion.12
  159.3 3.4 %squeeze.39 = bf16[192,3584]{1,0:T(8,128)(2,1)} reshape(bf16[1,16,1,12,3584]{4,3,2,0,1:T(8,128)(2,1)} %get-tuple-element.34) | data formatting | bytes 2752512 | tf_op jit(solution)/shard_map/squeeze | solution.py:108
  162.8 2.0 fusion.3
  164.8 2.1 multiply_convert_fusion.1
  166.9 0.7 fusion.2
  167.6 0.7 fusion.1
  168.3 0.3 pad_maximum_fusion
  168.8 8.5 %copy.146 = bf16[3,1792,128]{2,0,1:T(4,128)(2,1)S(1)} copy(bf16[3,1792,128]{2,1,0:T(8,128)(2,1)S(1)} %broadcast_select_fusion) | data formatting | bytes 2752512 | tf_op jit(solution)/shard_map/jit(_where)/select_n | solution.py:140
  177.4 24.4 %all_to_all.39 = bf16[3,1792,128]{2,0,1:T(4,128)(2,1)S(1)} all-to-all(bf16[3,1792,128]{2,0,1:T(4,128)(2,1)S(1)} %copy.146), channel_id=1, replica_groups=mesh['pipe'=2,'expert'=16] {'pipe'}, dimensions={1} | all-to-all | bytes 2752512 | tf_op jit(solution)/shard_map/all_to_all | solution.py:61
  202.0 1.2 reverse.3
  203.2 2.5 copy.148
  205.7 4.8 %all-to-all-start.4 = ((bf16[6,896,128]{2,1,0:T(8,128)(2,1)}), bf16[6,896,128]{2,1,0:T(8,128)(2,1)}, u32[]{:S(2)}, u32[]{:S(2)}) async-start(bf16[6,896,128]{2,1,0:T(8,128)(2,1)} %bitcast.52), calls=%async_computation.4 | async-start | bytes 2752512 | tf_op jit(solution)/shard_map/all_to_all | solution.py:61
  210.5 2.4 squeeze.35
  212.9 0.5 fusion.20
  213.4 3.2 convolution_convert_fusion
  216.6 3.3 %reshape.120 = bf16[16,12,3584]{2,1,0:T(8,128)(2,1)} reshape(bf16[192,3584]{1,0:T(8,128)(2,1)} %convolution_convert_fusion) | data formatting | bytes 2752512 | tf_op jit(solution)/shard_map/reshape | solution.py:47
  219.9 6.8 %all-to-all-done.4 = bf16[6,896,128]{2,1,0:T(8,128)(2,1)} async-done(((bf16[6,896,128]{2,1,0:T(8,128)(2,1)}), bf16[6,896,128]{2,1,0:T(8,128)(2,1)}, u32[]{:S(2)}, u32[]{:S(2)}) %all-to-all-start.4) | async-done | bytes 1376288 | tf_op jit(solution)/shard_map/all_to_all | solution.py:61
  226.6 6.7 %all-to-all-start.1 = ((bf16[16,12,3584]{2,1,0:T(8,128)(2,1)}), bf16[16,12,3584]{2,1,0:T(8,128)(2,1)}, u32[]{:S(2)}, u32[]{:S(2)}) async-start(bf16[16,12,3584]{2,1,0:T(8,128)(2,1)} %reshape.120), calls=%async_computation.1 | async-start | bytes 3670016 | tf_op jit(solution)/shard_map/all_to_all | solution.py:46
  233.3 0.5 fusion.16
  233.9 0.5 fusion
  234.4 1.4 reshape.123
  235.8 39.4 %all-to-all-done.1 = bf16[16,12,3584]{2,1,0:T(8,128)(2,1)} async-done(((bf16[16,12,3584]{2,1,0:T(8,128)(2,1)}), bf16[16,12,3584]{2,1,0:T(8,128)(2,1)}, u32[]{:S(2)}, u32[]{:S(2)}) %all-to-all-start.1) | async-done | bytes 1376288 | tf_op jit(solution)/shard_map/all_to_all | solution.py:46
  275.2 4.9 %all-to-all-start.2 = ((bf16[16,12,3584]{2,1,0:T(8,128)(2,1)}), bf16[16,12,3584]{2,1,0:T(8,128)(2,1)S(1)}, u32[]{:S(2)}, u32[]{:S(2)}) async-start(bf16[16,12,3584]{2,1,0:T(8,128)(2,1)} %reshape.123), calls=%async_computation.2 | async-start | bytes 3670016 | tf_op jit(solution)/shard_map/all_to_all | solution.py:46
  280.2 1.5 convert_bitcast_fusion
  281.9 1.6 copy-done.2
  283.5 0.4 fusion.6
  283.9 1.0 slice_bitcast_fusion
  284.9 1.0 copy.150
  285.9 1.8 bitcast_reduce_fusion.1
  287.8 34.2 %all-to-all-done.2 = bf16[16,12,3584]{2,1,0:T(8,128)(2,1)S(1)} async-done(((bf16[16,12,3584]{2,1,0:T(8,128)(2,1)}), bf16[16,12,3584]{2,1,0:T(8,128)(2,1)S(1)}, u32[]{:S(2)}, u32[]{:S(2)}) %all-to-all-start.2) | async-done | bytes 1376288 | tf_op jit(solution)/shard_map/all_to_all | solution.py:46
  322.0 0.3 bitcast_reduce_fusion
  322.3 0.8 fusion.5
  323.1 0.9 fusion.4
  (35 shorter events, 2.7 us)
Async XLA Ops:
  0.6 158.2 %copy-start = (bf16[1,3584,128]{2,1,0:T(8,128)(2,1)S(1)}, bf16[1,3584,128]{2,1,0:T(8,128)(2,1)}, u32[]{:S(2)}) copy-start(bf16[1,3584,128]{2,1,0:T(8,128)(2,1)} %param.18) | copy-start | bytes 2752516
  23.5 127.1 %all-to-all-start = ((bf16[16,3,1,12,3584]{4,3,2,1,0:T(8,128)(2,1)}), bf16[16,3,1,12,3584]{4,3,2,1,0:T(8,128)(2,1)}, u32[]{:S(2)}, u32[]{:S(2)}) async-start(bf16[16,3,1,12,3584]{4,3,2,1,0:T(8,128)(2,1)} %fusion.22), calls=%async_computation | async-start | bytes 11010048 | tf_op jit(solution)/shard_map/all_to_all | solution.py:12
  155.8 2.5 copy-start.3
  168.7 8.7 %copy-start.1 = (bf16[3,3584,128]{2,1,0:T(8,128)(2,1)}, bf16[3,3584,128]{2,1,0:T(8,128)(2,1)S(1)}, u32[]{:S(2)}) copy-start(bf16[3,3584,128]{2,1,0:T(8,128)(2,1)S(1)} %pad_maximum_fusion) | copy-start | bytes 8257540
  205.7 20.9 %all-to-all-start.4 = ((bf16[6,896,128]{2,1,0:T(8,128)(2,1)}), bf16[6,896,128]{2,1,0:T(8,128)(2,1)}, u32[]{:S(2)}, u32[]{:S(2)}) async-start(bf16[6,896,128]{2,1,0:T(8,128)(2,1)} %bitcast.52), calls=%async_computation.4 | async-start | bytes 2752512 | tf_op jit(solution)/shard_map/all_to_all | solution.py:61
  226.6 48.6 %all-to-all-start.1 = ((bf16[16,12,3584]{2,1,0:T(8,128)(2,1)}), bf16[16,12,3584]{2,1,0:T(8,128)(2,1)}, u32[]{:S(2)}, u32[]{:S(2)}) async-start(bf16[16,12,3584]{2,1,0:T(8,128)(2,1)} %reshape.120), calls=%async_computation.1 | async-start | bytes 3670016 | tf_op jit(solution)/shard_map/all_to_all | solution.py:46
  275.2 46.7 %all-to-all-start.2 = ((bf16[16,12,3584]{2,1,0:T(8,128)(2,1)}), bf16[16,12,3584]{2,1,0:T(8,128)(2,1)S(1)}, u32[]{:S(2)}, u32[]{:S(2)}) async-start(bf16[16,12,3584]{2,1,0:T(8,128)(2,1)} %reshape.123), calls=%async_computation.2 | async-start | bytes 3670016 | tf_op jit(solution)/shard_map/all_to_all | solution.py:46
  281.7 1.8 copy-start.2
